TPU v7x, 32 devices: a whole 2x2x4 slice. The times are simulated.
32 devices in a mesh: groups: 2 (over y), frame: 4 (over z), tok: 2 (over x), head: 2 (over core).
Axes of the slice: x: 2, y: 2, z: 4, core: 2. Of those that a mesh axis runs over, the one named last changes fastest.
Arguments:
- frames: bfloat16 [8, 1024, 1152], P(('groups', 'frame'), 'tok'), parts along dimension 0, may hold values from -6 to 6
- modulation: float32 [3, 1152], replicated, may hold values from -4.1 to 6, as said below
- w_qkv: bfloat16 [1152, 16, 3, 72], P('frame', 'head'), may hold values from -0.1875 to 0.1875
- w_out: bfloat16 [1152, 1152], P('head', 'frame'), may hold values from -0.1875 to 0.1875
- anchor_offsets: int32 [2], P('groups'), parts along dimension 0, may hold values from 0 to 3
Outputs:
- updated: bfloat16 [8, 1024, 1152], P(('groups', 'frame'), 'tok', 'head'), parts along dimension 0
There are 2 independent parts, one for each index of `groups`. A program takes and returns all parts, laid end to end along the dimension named above; an argument that names none is the same for every part. Nothing has to cross between parts.
Inputs may be any that keep to these rules, and one draw needn't show every extreme that they name: anchor_offsets[c] is the offset, within span c of 4 frames, of the frame that all frames of the span attend to. `modulation`: row 0 is the shift, row 1 the scale, row 2 the gate.
All inputs are finite; a program needn't handle non-finite values.
Results may differ from a plain program's by a relative error of at most 0.0049.
The roundings to bfloat16 on the way count: a program that leaves them out, or rounds other values in their place, can miss the bound.
Values may be sent and summed in bfloat16 or wider, within the bound.
A program may use at most 64 MiB of HBM per device.

v0:
```python
import math

import jax
import jax.numpy as jnp
from jax import lax
from jax.sharding import PartitionSpec as P


def shifted(block, axis, distance):
    devices = range(lax.axis_size(axis))
    route = [(i - distance, i) for i in devices if i - distance in devices]
    return lax.ppermute(block, axis, route)


def from_partner(block, axis, stride):
    count = lax.axis_size(axis)
    route = []
    for low in range(count):
        high = low | 1 << stride
        if high != low and high < count:
            route += [(low, high), (high, low)]
    return lax.ppermute(block, axis, route)


def attend(queries, kv_all, first_frame, anchor, head_dim):
    frame_count, query_rows, query_width = queries.shape
    key_count = kv_all.shape[1]
    head_count = query_width // head_dim
    block_rows = math.gcd(512, query_rows)
    kv_heads = kv_all.reshape(frame_count + 2, key_count, head_count, 2, head_dim)
    global_idx = first_frame + 0
    use_prev = global_idx > 0
    use_anchor = (anchor != global_idx) & (anchor != global_idx - 1)
    valid_keys = jnp.concatenate(
        [
            jnp.broadcast_to(use_anchor, (key_count,)),
            jnp.broadcast_to(use_prev, (key_count,)),
            jnp.ones((key_count,), bool),
        ]
    )
    frame_queries = queries[0]

    def one_head(head_idx):
        picked = lax.dynamic_index_in_dim(kv_heads, head_idx, 2, keepdims=False)
        key_rows = jnp.concatenate(
            [picked[frame_count + 1, :, 0], picked[frame_count, :, 0], picked[0, :, 0]], 0
        )
        val_rows = jnp.concatenate(
            [picked[frame_count + 1, :, 1], picked[frame_count, :, 1], picked[0, :, 1]], 0
        )
        query_head = lax.dynamic_slice_in_dim(frame_queries, head_idx * head_dim, head_dim, 1)
        query_blocks = query_head.reshape(query_rows // block_rows, block_rows, head_dim)

        def one_block(query_block):
            scores = lax.dot_general(
                query_block, key_rows, (((1,), (1,)), ((), ())), preferred_element_type=jnp.float32
            ) * head_dim ** (-0.5)
            scores = jnp.where(valid_keys[None, :], scores, -1e30)
            row_max = jnp.max(scores, axis=-1, keepdims=True)
            probs = jnp.exp(scores - row_max)
            denominator = jnp.sum(probs, axis=-1, keepdims=True)
            numerator = jnp.dot(
                probs.astype(jnp.bfloat16), val_rows, preferred_element_type=jnp.float32
            )
            return (numerator / denominator).astype(jnp.bfloat16)

        return lax.map(one_block, query_blocks).reshape(query_rows, head_dim)

    per_head = lax.map(one_head, jnp.arange(head_count, dtype=jnp.int32))
    frame_outputs = [jnp.transpose(per_head, (1, 0, 2)).reshape(query_rows, head_count * head_dim)]
    return jnp.stack(frame_outputs)


def on_device(frames, modulation, w_qkv, w_out, anchor_offsets):
    frame_count, row_count, model_width = frames.shape
    head_local = w_qkv.shape[1]
    head_dim = w_qkv.shape[3]
    my_index = lax.axis_index("frame")
    flat_rows = frames.reshape(frame_count * row_count, model_width).astype(jnp.float32)
    row_mean = jnp.mean(flat_rows, axis=-1, keepdims=True)
    centred = flat_rows - row_mean
    row_var = jnp.mean(centred * centred, axis=-1, keepdims=True)
    normed = centred * lax.rsqrt(row_var + 1e-06)
    hidden = (normed * (1.0 + modulation[1]) + modulation[0]).astype(jnp.bfloat16)
    full_weight = lax.all_gather(w_qkv, "frame", axis=0, tiled=True)
    mixed = jnp.dot(
        hidden,
        full_weight.reshape(model_width, head_local * 3 * head_dim),
        preferred_element_type=jnp.float32,
    )
    mixed = mixed.astype(jnp.bfloat16).reshape(frame_count, row_count, head_local, 3, head_dim)
    queries = mixed[:, :, :, 0, :].reshape(frame_count, row_count, head_local * head_dim)
    keyvals = mixed[:, :, :, 1:, :].reshape(frame_count, row_count, head_local * 2 * head_dim)
    span_count = anchor_offsets.shape[0]
    total_frames = frame_count * lax.axis_size("frame")
    span_len = total_frames // span_count
    first_frame = my_index * frame_count
    mine_span = first_frame // span_len
    anchor = mine_span * span_len + anchor_offsets[mine_span]
    prev_kv = shifted(keyvals[frame_count - 1], "frame", 1)
    holder = anchor // frame_count
    anchor_kv = lax.dynamic_index_in_dim(keyvals, anchor % frame_count, 0, keepdims=False)
    levels = (span_len // frame_count).bit_length() - 1
    for bit_index in range(levels):
        partner = from_partner(anchor_kv, "frame", bit_index)
        take_partner = my_index >> bit_index & 1 != holder >> bit_index & 1
        anchor_kv = jnp.where(take_partner, partner, anchor_kv)
    kv_all = jnp.concatenate([keyvals, prev_kv[None], anchor_kv[None]], 0)
    kv_whole = lax.all_gather(kv_all, "tok", axis=1, tiled=True)
    attended = attend(queries, kv_whole, first_frame, anchor, head_dim)
    flat_attended = attended.reshape(frame_count * row_count, head_local * head_dim)
    term_cols = jnp.dot(
        flat_attended,
        lax.all_gather(w_out, "frame", axis=1, tiled=True),
        preferred_element_type=jnp.float32,
    )
    summed = lax.psum_scatter(term_cols, "head", scatter_dimension=1, tiled=True)
    half_width = summed.shape[1]
    col_start = lax.axis_index("head") * half_width
    residual_in = lax.dynamic_slice_in_dim(flat_rows, col_start, half_width, 1)
    gate_part = lax.dynamic_slice_in_dim(modulation[2], col_start, half_width, 0)
    result = (residual_in + gate_part * summed).astype(jnp.bfloat16)
    return result.reshape(frame_count, row_count, half_width)


def solution(mesh):
    placed = (
        P(("groups", "frame"), "tok", None),
        P(),
        P("frame", "head", None, None),
        P("head", "frame"),
        P("groups"),
    )
    return jax.shard_map(
        on_device,
        mesh=mesh,
        in_specs=placed,
        out_specs=P(("groups", "frame"), "tok", "head"),
        check_vma=False,
    )
```

profile of v0, /device:TPU:0, one launch (start us, length us, event | category | flops | bytes accessed | tf_op | source)
XLA Modules:
  0.0 445.5 jit_solution(5562761133376638567)
XLA Ops:
  6.5 3.9 copy.20
  10.5 0.2 convert_reduce_fusion
  10.8 0.5 fusion.36
  11.3 130.3 %all-gather.4.cloned.1.call-done = bf16[1152,8,3,72]{3,1,2,0:T(8,128)(2,1)} async-done(((bf16[288,8,3,72]{3,1,2,0:T(8,128)(2,1)}), bf16[1152,8,3,72]{3,1,2,0:T(8,128)(2,1)}) %all-gather.4.cloned.1.call-update) | async-done | bytes 3981328 | tf_op jit(solution)/shard_map/all_gather | solution.py:85
  141.5 9.3 %copy.21 = bf16[1152,8,3,72]{0,3,2,1:T(8,128)(2,1)} copy(bf16[1152,8,3,72]{3,1,2,0:T(8,128)(2,1)} %all-gather.4.cloned.1.call-done) | data formatting | bytes 7962624 | tf_op jit(solution)/shard_map/all_gather | solution.py:85
  150.9 4.8 %convolution_convert_fusion = bf16[512,1728]{0,1:T(8,128)(2,1)S(1)} fusion(bf16[1152,1728]{0,1:T(8,128)(2,1)} %bitcast.65, bf16[1,512,1152]{2,1,0:T(8,128)(2,1)S(1)} %copy-done, f32[1152]{0:T(1024)S(1)} %get-tuple-element.75, f32[1152]{0:T(1024)S(1)} %get-tuple-element.74, f32[512]{0:T(512)S(1)} %add_rsqrt_fusion, f32[512]{0:T(512)S(1)} %broadcast_multiply_fusion), kind=kOutput, calls=%fused_computation.36 | convolution fusion | flops 2042855424 | bytes 6943744 | tf_op jit(solution)/shard_map/dot_general | solution.py:86
  155.8 1.1 copy-done.1
  157.6 27.3 %collective-permute-done.1 = bf16[512,1152]{0,1:T(8,128)(2,1)} collective-permute-done((bf16[512,1152]{0,1:T(8,128)(2,1)S(1)}, bf16[512,1152]{0,1:T(8,128)(2,1)}, u32[]{:S(2)}, u32[]{:S(2)}) %collective-permute-start.1) | collective-permute-done | bytes 1179680 | tf_op jit(solution)/shard_map/ppermute | solution.py:22
  184.9 1.4 broadcast_select_fusion
  186.3 0.3 collective-permute-start.2
  186.6 2.3 collective-permute-start
  188.9 49.5 %collective-permute-done.2 = bf16[512,1152]{0,1:T(8,128)(2,1)} collective-permute-done((bf16[512,1152]{0,1:T(8,128)(2,1)S(1)}, bf16[512,1152]{0,1:T(8,128)(2,1)}, u32[]{:S(2)}, u32[]{:S(2)}) %collective-permute-start.2) | collective-permute-done | bytes 1179680 | tf_op jit(solution)/shard_map/ppermute | solution.py:22
  238.5 1.4 select_bitcast_fusion
  239.9 3.0 pad_maximum_fusion
  243.0 0.7 all-gather.8.cloned.1.call-update
  243.8 1.1 slice.44
  244.9 108.5 %all-gather.6.cloned.1.call-done = bf16[3,1024,1152]{1,2,0:T(8,128)(2,1)} async-done(((bf16[3,512,1152]{1,2,0:T(8,128)(2,1)}), bf16[3,1024,1152]{1,2,0:T(8,128)(2,1)}) %all-gather.6.cloned.1.call-update) | async-done | bytes 7077904 | tf_op jit(solution)/shard_map/all_gather | solution.py:109
  353.4 69.1 %while.10 = (s32[]{:T(128)}, bf16[8,512,72]{1,2,0:T(8,128)(2,1)S(1)}, pred[3072]{0:T(1024)(128)(4,1)S(1)}, s32[8]{0:T(128)S(1)}, bf16[512,576]{0,1:T(8,128)(2,1)...) while((s32[]{:T(128)}, ...), condition=%wide.region_5.6_spmd, body=%wide.region_2.5_spmd.sunk | while | flops 473013248 | bytes 23465172 | solution.py:69
  353.4 0.6 dynamic_slice.40
  355.9 1.2 dynamic-slice_bitcast_fusion.2
  357.8 1.3 fusion.56
  359.1 1.4 fusion.57
  360.5 1.5 fusion.58
  362.0 0.6 dynamic_slice.40
  364.5 1.2 dynamic-slice_bitcast_fusion.2
  366.5 1.3 fusion.56
  367.7 1.4 fusion.57
  369.2 1.5 fusion.58
  370.7 0.6 dynamic_slice.40
  373.2 1.2 dynamic-slice_bitcast_fusion.2
  375.1 1.3 fusion.56
  376.4 1.4 fusion.57
  377.8 1.5 fusion.58
  379.3 0.6 dynamic_slice.40
  381.8 1.2 dynamic-slice_bitcast_fusion.2
  383.8 1.2 fusion.56
  385.0 1.4 fusion.57
  386.5 1.5 fusion.58
  388.0 0.6 dynamic_slice.40
  390.5 1.2 dynamic-slice_bitcast_fusion.2
  392.4 1.2 fusion.56
  393.7 1.4 fusion.57
  395.1 1.5 fusion.58
  396.6 0.6 dynamic_slice.40
  399.1 1.2 dynamic-slice_bitcast_fusion.2
  401.1 1.2 fusion.56
  402.3 1.4 fusion.57
  403.7 1.5 fusion.58
  405.2 0.6 dynamic_slice.40
  407.8 1.2 dynamic-slice_bitcast_fusion.2
  409.7 1.2 fusion.56
  411.0 1.4 fusion.57
  412.4 1.5 fusion.58
  413.9 0.6 dynamic_slice.40
  416.4 1.2 dynamic-slice_bitcast_fusion.2
  418.4 1.2 fusion.56
  419.6 1.4 fusion.57
  421.0 1.5 fusion.58
  422.5 3.9 fusion.45
  426.4 0.2 convert_element_type.27
  426.6 1.5 constant_dynamic-slice_fusion
  428.1 1.7 copy.19
  429.9 6.8 %reduce-scatter.2.cloned.1.call-done = f32[512,576]{0,1:T(8,128)} async-done(((f32[512,1152]{0,1:T(8,128)}), f32[512,576]{0,1:T(8,128)}) %reduce-scatter.2.cloned.1.call-update) | async-done | bytes 1179664 | tf_op jit(solution)/shard_map/reduce_scatter | solution.py:117
  436.7 2.3 fusion.44
  (34 shorter events, 1.0 us)
Async XLA Ops:
  6.5 135.0 %all-gather.4.cloned.1.call-start = ((), (), s32[]{:S(2)}) async-start(), calls=%async_computation.1 | async-start | bytes 8847360 | tf_op jit(solution)/shard_map/all_gather | solution.py:85
  6.5 4.0 copy-start
  10.5 0.8 copy-start.2
  10.5 342.9 %all-gather.6.cloned.1.call-start = ((), (), s32[]{:S(2)}) async-start(), calls=%async_computation.2 | async-start | bytes 10616832 | tf_op jit(solution)/shard_map/all_gather | solution.py:109
  155.7 1.2 copy-start.1
  156.9 28.0 %collective-permute-start.1 = (bf16[512,1152]{0,1:T(8,128)(2,1)S(1)}, bf16[512,1152]{0,1:T(8,128)(2,1)}, u32[]{:S(2)}, u32[]{:S(2)}) collective-permute-start(bf16[512,1152]{0,1:T(8,128)(2,1)S(1)} %bitcast.62), channel_id=1, source_target_pairs={{0,4},{4,0},{8,12},{12,8},{1,5},{5,1},{9,13},{13,9},{2,6},{6,2},{1... | collective-permute-start | bytes 3538952 | tf_op jit(solution)/shard_map/ppermute | solution.py:22
  186.3 52.2 %collective-permute-start.2 = (bf16[512,1152]{0,1:T(8,128)(2,1)S(1)}, bf16[512,1152]{0,1:T(8,128)(2,1)}, u32[]{:S(2)}, u32[]{:S(2)}) collective-permute-start(bf16[512,1152]{0,1:T(8,128)(2,1)S(1)} %broadcast_select_fusion), channel_id=1, source_target_pairs={{0,8},{8,0},{4,12},{12,4},{1,9},{9,1},{5,13},{13,5},{2,10},{10,2},... | collective-permute-start | bytes 3538952 | tf_op jit(solution)/shard_map/ppermute | solution.py:22
  186.6 53.2 %collective-permute-start = (bf16[512,1152]{0,1:T(8,128)(2,1)S(1)}, bf16[512,1152]{0,1:T(8,128)(2,1)}, u32[]{:S(2)}, u32[]{:S(2)}) collective-permute-start(bf16[512,1152]{0,1:T(8,128)(2,1)S(1)} %bitcast.63), channel_id=1, source_target_pairs={{0,4},{4,8},{8,12},{1,5},{5,9},{9,13},{2,6},{6,10},{10,14},{3,7},{... | collective-permute-start | bytes 3538952 | tf_op jit(solution)/shard_map/ppermute | solution.py:12
  242.9 179.6 %all-gather.8.cloned.1.call-start = ((), (), s32[]{:S(2)}) async-start(), calls=%async_computation.3 | async-start | bytes 1843200 | tf_op jit(solution)/shard_map/all_gather | solution.py:114
  243.7 193.0 %reduce-scatter.2.cloned.1.call-start = ((), (), s32[]{:S(2)}) async-start(), calls=%async_computation.4 | async-start | bytes 3538944 | tf_op jit(solution)/shard_map/reduce_scatter | solution.py:117
Sparse Core Ops, SparseCore 0:
  10.6 130.8 all-gather.3
  243.0 110.2 all-gather.5
  354.9 35.3 all-gather.7
  426.6 10.0 reduce-scatter.1
where the time goes:
time: 447 us; the launch traced here: 445 us
  waiting for transfers between devices  323 us (72%)
  local copies, waits for them, and re-layouts  34.2 us (8%)
  matrix products  30.4 us (7%)
  loops' own time  20.6 us (5%)
  other arithmetic  20.4 us (5%)
  between operations  14 us (3%)
    all_gather x1, waiting for transfers between devices, on_device(): full_weight = lax.all_gather(w_qkv, 'frame', axis=0, tiled=True)  130 us
    all_gather x1, waiting for transfers between devices, on_device(): kv_whole = lax.all_gather(kv_all, 'tok', axis=1, tiled=True)  108 us
    ppermute x2, waiting for transfers between devices, from_partner(): return lax.ppermute(block, axis, route)  76.9 us
    another operation x1, loops' own time, attend(): per_head = lax.map(one_head, jnp.arange(head_count, dtype=jnp.int32))  20.6 us
    dot_general x8, matrix products, one_block(): jnp.dot(probs.astype(jnp.bfloat16), val_rows, preferred_element_type=jnp....  11.8 us
    reduce_sum x8, other arithmetic, one_block(): denominator = jnp.sum(probs, axis=-1, keepdims=True)  11.4 us
    dot_general x8, matrix products, one_block(): lax.dot_general(query_block, key_rows, (((1,), (1,)), ((), ())), preferre...  10 us
    squeeze x8, local copies, waits for them, and re-layouts, one_head(): picked = lax.dynamic_index_in_dim(kv_heads, head_idx, 2, keepdims=False)  9.88 us
  transfers between devices with their start and end apart: 7, of which 5 were waited for; matrix products, arithmetic and copies ran while one was open for 12% of the time, Pallas kernels for 0%

commit v1 on v0

--- a/solution.py
+++ b/solution.py
@@ -1,8 +1,11 @@
+import functools
 import math
 
 import jax
 import jax.numpy as jnp
 from jax import lax
+from jax.experimental import pallas as pl
+from jax.experimental.pallas import tpu as pltpu
 from jax.sharding import PartitionSpec as P
 
 
@@ -71,7 +74,7 @@
     return jnp.stack(frame_outputs)
 
 
-def on_device(frames, modulation, w_qkv, w_out, anchor_offsets):
+def on_device_rings(frames, modulation, w_qkv, w_out, anchor_offsets):
     frame_count, row_count, model_width = frames.shape
     head_local = w_qkv.shape[1]
     head_dim = w_qkv.shape[3]
@@ -123,6 +126,351 @@
     return result.reshape(frame_count, row_count, half_width)
 
 
+MESH = pl.DeviceIdType.MESH
+
+
+def remote(src, dst, send_sem, recv_sem, **where):
+    return pltpu.make_async_remote_copy(
+        src_ref=src,
+        dst_ref=dst,
+        send_sem=send_sem,
+        recv_sem=recv_sem,
+        device_id=where,
+        device_id_type=MESH,
+    )
+
+
+def greet(peers):
+    barrier = pltpu.get_barrier_semaphore()
+    for peer in peers:
+        pl.semaphore_signal(barrier, inc=1, device_id=peer, device_id_type=MESH)
+    pl.semaphore_wait(barrier, len(peers))
+
+
+def gather_kernel(
+    nz, h_ref, w_ref, wo_ref, h_all, w_all, wo_all,
+    local_sem, h_send, h_fwd, h_core, h_recv, w_send, w_fwd, w_recv, o_send, o_fwd, o_recv, o_own,
+):
+    y, z = lax.axis_index("groups"), lax.axis_index("frame")
+    x, c = lax.axis_index("tok"), lax.axis_index("head")
+    per_core = nz // 2
+    quarter = h_ref.shape[0] // 2
+    home = z // per_core
+    slot = z % per_core
+    others = [lax.rem(z + step, nz) for step in range(1, nz)]
+
+    locals_ = [
+        pltpu.make_async_copy(h_ref, h_all.at[z, pl.ds(x * 2 * quarter, 2 * quarter)], local_sem.at[0]),
+        pltpu.make_async_copy(w_ref, w_all.at[z], local_sem.at[1]),
+    ]
+    for copy in locals_:
+        copy.start()
+    own_out = pltpu.make_async_copy(wo_ref, wo_all.at[slot, c], local_sem.at[2])
+
+    @pl.when(home == c)
+    def _():
+        own_out.start()
+
+    greet(
+        [{"frame": other, "head": core} for other in others for core in (0, 1)]
+        + [{"head": 1 - c}, {"tok": 1 - x}, {"groups": 1 - y}]
+    )
+
+    def piece(frame, tok, core):
+        return h_all.at[frame, pl.ds((tok * 2 + core) * quarter, quarter)]
+
+    mine = h_ref.at[pl.ds(c * quarter, quarter)]
+    sends = []
+    for k, other in enumerate(others):
+        sends.append(remote(mine, piece(z, x, c), h_send.at[k], h_recv.at[z, x, c], frame=other))
+        sends[-1].start()
+    sends.append(remote(mine, piece(z, x, c), h_send.at[nz - 1], h_recv.at[z, x, c], tok=1 - x))
+    sends[-1].start()
+    for k, other in enumerate(others):
+        sends.append(remote(w_ref.at[y], w_all.at[z, y], w_send.at[k], w_recv.at[z, y], frame=other))
+        sends[-1].start()
+    for k, other in enumerate(others):
+        sends.append(
+            remote(wo_ref.at[y], wo_all.at[slot, c, y], o_send.at[k], o_recv.at[slot, c, y], frame=other, head=home)
+        )
+        sends[-1].start()
+    over = remote(wo_ref, wo_all.at[slot, c], o_send.at[nz - 1], o_own, head=1 - c)
+
+    @pl.when(home != c)
+    def _():
+        over.start()
+
+    def arrived(ref, sem):
+        remote(ref, ref, h_send.at[0], sem, head=1 - c).wait_recv()
+
+    for k, other in enumerate(others):
+        got = piece(other, x, c)
+        arrived(got, h_recv.at[other, x, c])
+        sends.append(remote(got, got, h_fwd.at[k], h_recv.at[other, x, c], tok=1 - x))
+        sends[-1].start()
+        sends.append(remote(got, got, h_core.at[0, k], h_recv.at[other, x, c], head=1 - c))
+        sends[-1].start()
+        part = w_all.at[other, y]
+        arrived(part, w_recv.at[other, y])
+        sends.append(remote(part, part, w_fwd.at[k], w_recv.at[other, y], groups=1 - y))
+        sends[-1].start()
+    for i in range(per_core):
+        for core in (0, 1):
+            block = wo_all.at[i, core, y]
+            onward = remote(block, block, o_fwd.at[i, core], o_recv.at[i, core, y], groups=1 - y)
+
+            @pl.when(c * per_core + i != z)
+            def _():
+                arrived(block, o_recv.at[i, core, y])
+                onward.start()
+
+    for k, frame in enumerate([z] + others):
+        got = piece(frame, 1 - x, c)
+        arrived(got, h_recv.at[frame, 1 - x, c])
+        sends.append(remote(got, got, h_core.at[1, k], h_recv.at[frame, 1 - x, c], head=1 - c))
+        sends[-1].start()
+    for other in others:
+        arrived(w_all.at[other, 1 - y], w_recv.at[other, 1 - y])
+        arrived(piece(other, x, 1 - c), h_recv.at[other, x, 1 - c])
+    for frame in [z] + others:
+        arrived(piece(frame, 1 - x, 1 - c), h_recv.at[frame, 1 - x, 1 - c])
+    for i in range(per_core):
+        for core in (0, 1):
+            block = wo_all.at[i, core, y]
+            onward = remote(block, block, o_fwd.at[i, core], o_recv.at[i, core, y], groups=1 - y)
+
+            @pl.when(c * per_core + i != z)
+            def _():
+                arrived(wo_all.at[i, core, 1 - y], o_recv.at[i, core, 1 - y])
+                onward.wait_send()
+
+    @pl.when(home == c)
+    def _():
+        arrived(wo_all.at[slot, 1 - c], o_own)
+        own_out.wait()
+
+    @pl.when(home != c)
+    def _():
+        over.wait_send()
+
+    for copy in locals_:
+        copy.wait()
+    for copy in sends:
+        copy.wait_send()
+
+
+def gather(hidden, weight, out_weight, nz):
+    rows, width = hidden.shape
+    dma = pltpu.SemaphoreType.DMA
+    vmem, anywhere = pl.BlockSpec(memory_space=pltpu.VMEM), pl.BlockSpec(memory_space=pl.ANY)
+    return pl.pallas_call(
+        functools.partial(gather_kernel, nz),
+        out_shape=(
+            jax.ShapeDtypeStruct((nz, 2 * rows, width), hidden.dtype),
+            jax.ShapeDtypeStruct((nz,) + weight.shape, weight.dtype),
+            jax.ShapeDtypeStruct((nz // 2, 2) + out_weight.shape, out_weight.dtype),
+        ),
+        in_specs=[vmem] * 3,
+        out_specs=(anywhere,) * 3,
+        scratch_shapes=[
+            dma((3,)),
+            dma((nz,)),
+            dma((nz - 1,)),
+            dma((2, nz)),
+            dma((nz, 2, 2)),
+            dma((nz - 1,)),
+            dma((nz - 1,)),
+            dma((nz, 2)),
+            dma((nz,)),
+            dma((nz // 2, 2)),
+            dma((nz // 2, 2, 2)),
+            dma,
+        ],
+        compiler_params=pltpu.CompilerParams(collective_id=0, has_side_effects=True),
+        name="gather",
+    )(hidden, weight, out_weight)
+
+
+def attend_kernel(heads, hd, chunk, pick, anc_ref, prev_ref, own_ref, w_ref, o_ref, wide, keys, vals, queries):
+    step = pl.program_id(0)
+    frame_rows = own_ref.shape[1]
+    lanes = keys.shape[2]
+
+    @pl.when(step == 0)
+    def _():
+        wide[...] = jnp.zeros_like(wide)
+        for head in range(heads):
+            for what in range(3):
+                place = ((what + 2) % 3 * heads + head) * lanes
+                wide[:, place : place + hd] = w_ref[:, (head * 3 + what) * hd : (head * 3 + what + 1) * hd]
+
+        def project(ref, at, columns, targets, base):
+            here = pl.ds(pl.multiple_of(at * chunk, chunk), chunk)
+            there = pl.ds(pl.multiple_of(base + at * chunk, chunk), chunk)
+            mixed = jnp.dot(ref[0, here, :], wide[:, columns], preferred_element_type=jnp.float32)
+            mixed = mixed.astype(jnp.bfloat16)
+            for t, target in enumerate(targets):
+                for head in range(heads):
+                    place = (t * heads + head) * lanes
+                    target[head, there, :] = mixed[:, place : place + lanes]
+
+        both = slice(0, 2 * heads * lanes)
+        for block, ref in enumerate((anc_ref, prev_ref, own_ref)):
+
+            @pl.loop(0, frame_rows // chunk)
+            def _(at):
+                project(ref, at, both, (keys, vals), block * frame_rows)
+
+        @pl.loop(0, frame_rows // chunk)
+        def _(at):
+            project(own_ref, at, slice(2 * heads * lanes, 3 * heads * lanes), (queries,), 0)
+
+    rate = hd ** (-0.5) * math.log2(math.e)
+    offsets = [jnp.where(pick[3 + k] == 1, 0.0, -1e30).astype(jnp.float32) for k in range(2)] + [0.0]
+    rows = o_ref.shape[0]
+    here = pl.ds(pl.multiple_of(step * rows, rows), rows)
+    for head in range(heads):
+        query = queries[head, here, :]
+        scores = [
+            lax.dot_general(
+                query,
+                keys[head, k * frame_rows : (k + 1) * frame_rows, :],
+                (((1,), (1,)), ((), ())),
+                preferred_element_type=jnp.float32,
+            )
+            for k in range(3)
+        ]
+        tops = [jnp.max(s, axis=-1, keepdims=True) + offset for s, offset in zip(scores, offsets)]
+        top = jnp.maximum(jnp.maximum(tops[0], tops[1]), tops[2])
+        denominator, numerator = 0.0, 0.0
+        for k in range(3):
+            probs = jnp.exp2((scores[k] - (top - offsets[k])) * rate)
+            denominator += jnp.sum(probs, axis=-1, keepdims=True)
+            numerator += jnp.dot(
+                probs.astype(jnp.bfloat16),
+                vals[head, k * frame_rows : (k + 1) * frame_rows, :],
+                preferred_element_type=jnp.float32,
+            )
+        result = (numerator / denominator).astype(jnp.bfloat16)
+        o_ref[:, head * hd : (head + 1) * hd] = result[:, :hd]
+
+
+def attend_heads(pick, h_all, weight, heads, hd):
+    _, frame_rows, width = h_all.shape
+    lanes = -(-hd // 128) * 128
+    block_rows = math.gcd(256, frame_rows)
+
+    def frame_block(which):
+        return pl.BlockSpec((1, frame_rows, width), lambda i, pick: (pick[which], 0, 0))
+
+    return pl.pallas_call(
+        functools.partial(attend_kernel, heads, hd, block_rows),
+        out_shape=jax.ShapeDtypeStruct((frame_rows, heads * hd), jnp.bfloat16),
+        grid_spec=pltpu.PrefetchScalarGridSpec(
+            num_scalar_prefetch=1,
+            grid=(frame_rows // block_rows,),
+            in_specs=[frame_block(2), frame_block(1), frame_block(0), pl.BlockSpec(weight.shape, lambda i, pick: (0, 0))],
+            out_specs=pl.BlockSpec((block_rows, heads * hd), lambda i, pick: (i, 0)),
+            scratch_shapes=[
+                pltpu.VMEM((width, 3 * heads * lanes), jnp.bfloat16),
+                pltpu.VMEM((heads, 3 * frame_rows, lanes), jnp.bfloat16),
+                pltpu.VMEM((heads, 3 * frame_rows, lanes), jnp.bfloat16),
+                pltpu.VMEM((heads, frame_rows, lanes), jnp.bfloat16),
+            ],
+        ),
+        compiler_params=pltpu.CompilerParams(vmem_limit_bytes=56 * 1024 * 1024),
+        name="attend",
+    )(pick, h_all, h_all, h_all, weight)
+
+
+def output_kernel(per_core, att_ref, wo_ref, res_ref, gate_ref, o_ref, held, send, recv):
+    x, c = lax.axis_index("tok"), lax.axis_index("head")
+    rows = o_ref.shape[0]
+    greet([{"tok": 1 - x}, {"head": 1 - c}])
+    mine = att_ref.at[pl.ds(pl.multiple_of(x * rows, rows), rows)]
+    theirs = att_ref.at[pl.ds(pl.multiple_of((1 - x) * rows, rows), rows)]
+    across = remote(theirs, held.at[0], send.at[0], recv.at[0], tok=1 - x)
+    beside = remote(mine, held.at[1], send.at[1], recv.at[1], head=1 - c)
+    relay = remote(held.at[0], held.at[2], send.at[2], recv.at[2], head=1 - c)
+    across.start()
+    beside.start()
+
+    def term(block, core, tok):
+        return [
+            jnp.dot(block, wo_ref[i, core, tok], preferred_element_type=jnp.float32) for i in range(per_core)
+        ]
+
+    def plus(a, b):
+        return [p + q for p, q in zip(a, b)]
+
+    total = term(att_ref[pl.ds(pl.multiple_of(x * rows, rows), rows), :], c, x)
+    beside.wait_recv()
+    total = plus(total, term(held[1], 1 - c, x))
+    across.wait_recv()
+    relay.start()
+    total = plus(total, term(held[0], c, 1 - x))
+    relay.wait_recv()
+    total = plus(total, term(held[2], 1 - c, 1 - x))
+    width = wo_ref.shape[-1]
+    for i in range(per_core):
+        columns = slice(i * width, (i + 1) * width)
+        o_ref[:, columns] = (res_ref[:, columns].astype(jnp.float32) + gate_ref[:, columns] * total[i]).astype(o_ref.dtype)
+    across.wait_send()
+    beside.wait_send()
+    relay.wait_send()
+
+
+def project_out(attended, out_weight, residual, gate):
+    rows, columns = residual.shape
+    dma = pltpu.SemaphoreType.DMA
+    return pl.pallas_call(
+        functools.partial(output_kernel, out_weight.shape[0]),
+        out_shape=jax.ShapeDtypeStruct((rows, columns), jnp.bfloat16),
+        in_specs=[pl.BlockSpec(memory_space=pltpu.VMEM)] * 4,
+        out_specs=pl.BlockSpec(memory_space=pltpu.VMEM),
+        scratch_shapes=[pltpu.VMEM((3, rows, attended.shape[1]), jnp.bfloat16), dma((3,)), dma((3,))],
+        compiler_params=pltpu.CompilerParams(collective_id=1, has_side_effects=True),
+        name="project_out",
+    )(attended, out_weight, residual, gate)
+
+
+def on_device(frames, modulation, w_qkv, w_out, anchor_offsets, mesh_shape):
+    frame_count, row_count, model_width = frames.shape
+    depth, head_local, _, head_dim = w_qkv.shape
+    nz = mesh_shape["frame"]
+    pairs = all(mesh_shape[axis] == 2 for axis in ("groups", "tok", "head"))
+    if not (pairs and frame_count == 1 and anchor_offsets.shape[0] == 1 and nz % 2 == 0 and nz <= 4):
+        return on_device_rings(frames, modulation, w_qkv, w_out, anchor_offsets)
+    z, x, c = lax.axis_index("frame"), lax.axis_index("tok"), lax.axis_index("head")
+    rows = frames[0]
+    values = rows.astype(jnp.float32)
+    row_mean = jnp.mean(values, axis=-1, keepdims=True)
+    centred = values - row_mean
+    row_var = jnp.mean(centred * centred, axis=-1, keepdims=True)
+    normed = centred * lax.rsqrt(row_var + 1e-06)
+    hidden = (normed * (1.0 + modulation[1]) + modulation[0]).astype(jnp.bfloat16)
+    heads = head_local // 2
+    weight = lax.dynamic_slice_in_dim(w_qkv, x * heads, heads, 1)
+    weight = weight.reshape(2, depth // 2, heads * 3 * head_dim)
+    out_weight = w_out.reshape(2, w_out.shape[0] // 2, w_out.shape[1])
+    h_all, w_all, wo_all = gather(hidden, weight, out_weight, nz)
+    anchor = anchor_offsets[0]
+    pick = jnp.stack(
+        [
+            z,
+            jnp.maximum(z - 1, 0),
+            anchor,
+            ((anchor != z) & (anchor != z - 1)).astype(jnp.int32),
+            (z > 0).astype(jnp.int32),
+        ]
+    ).astype(jnp.int32)
+    attended = attend_heads(pick, h_all, w_all.reshape(model_width, heads * 3 * head_dim), heads, head_dim)
+    half_width = model_width // 2
+    residual = lax.dynamic_slice_in_dim(rows, c * half_width, half_width, 1)
+    gate = lax.dynamic_slice_in_dim(modulation[2:3], c * half_width, half_width, 1)
+    return project_out(attended, wo_all, residual, gate)[None]
+
+
 def solution(mesh):
     placed = (
         P(("groups", "frame"), "tok", None),
@@ -132,7 +480,7 @@
         P("groups"),
     )
     return jax.shard_map(
-        on_device,
+        functools.partial(on_device, mesh_shape=dict(mesh.shape)),
         mesh=mesh,
         in_specs=placed,
         out_specs=P(("groups", "frame"), "tok", "head"),

time: 447 us -> 191 us (0.43)
  the two profiles are of different devices: /device:TPU:0 before, /device:TPU:9 now
where the time goes in v1:
time: 191 us
  Pallas kernels  176 us (92%)
  local copies, waits for them, and re-layouts  11.6 us (6%)
  other arithmetic  2.26 us (1%)
    pallas_call x1, Pallas kernels, gather(): pl.pallas_call(functools.partial(gather_kernel, nz), out_shape=(jax.Shape...  122 us
    pallas_call x1, Pallas kernels, attend_heads(): pl.pallas_call(functools.partial(attend_kernel, heads, hd, block_rows), o...  38 us
    pallas_call x1, Pallas kernels, project_out(): pl.pallas_call(functools.partial(output_kernel, out_weight.shape[0]), out...  16.4 us
    reshape x2, local copies, waits for them, and re-layouts, on_device(): weight = weight.reshape(2, depth // 2, heads * 3 * head_dim)  5.04 us

profile of v1, /device:TPU:9, one launch (start us, length us, event | category | flops | bytes accessed | tf_op | source)
XLA Modules:
  0.0 190.8 jit_solution(12649893128965977152)
XLA Ops:
  0.0 0.0 copy-start
  0.0 0.0 copy-start.3
  0.0 0.0 copy-start.1
  0.8 0.7 stack.27.pick
  1.5 0.0 copy-done
  1.5 0.9 constant_dynamic-slice_fusion.1
  2.4 2.8 %reshape.23 = bf16[2,144,864]{1,0,2:T(2,128)(2,1)S(1)} reshape(bf16[288,4,3,72]{0,3,2,1:T(8,128)(2,1)} %constant_dynamic-slice_fusion.1) | data formatting | bytes 995328 | tf_op jit(solution)/shard_map/reshape | solution.py:454
  5.2 2.2 %copy.10.w_ref = bf16[2,144,864]{2,1,0:T(8,128)(2,1)} copy(bf16[2,144,864]{1,0,2:T(2,128)(2,1)S(1)} %reshape.23) | data formatting | bytes 995328 | tf_op jit(solution)/shard_map/reshape | solution.py:454
  7.5 0.0 copy-done.3
  7.5 0.0 copy-done.1
  7.5 0.0 copy-start.2
  7.5 0.2 convert_reduce_fusion
  7.7 0.5 fusion.3
  8.2 1.5 fusion.6.h_ref
  9.7 0.0 copy-done.2
  9.7 1.0 copy.9
  10.7 121.7 %gather.1 = (bf16[4,1024,1152]{2,1,0:T(8,128)(2,1)}, bf16[4,2,144,864]{3,2,1,0:T(8,128)(2,1)}, bf16[2,2,2,288,288]{4,3,2,1,0:T(8,128)(2,1)}) custom-call(bf16[512,1152]{1,0:T(8,128)(2,1)} %fusion.6.h_ref, bf16[2,144,864]{2,1,0:T(8,128)(2,1)} %copy.10.w_ref, bf16[2,288,288]{2,1,0:T(8,128)(2,1)} %bitcast.34), custom_call_target="tpu_custom_call" | custom-call | tf_op jit(solution)/shard_map/gather/pallas_call | solution.py:266
  132.5 38.0 %attend.1.att_ref = bf16[1024,288]{1,0:T(8,128)(2,1)} custom-call(s32[5]{0:T(128)} %stack.27.pick, bf16[4,1024,1152]{2,1,0:T(8,128)(2,1)} %get-tuple-element.8.anc_ref.prev_ref.own_ref, bf16[4,1024,1152]{2,1,0:T(8,128)(2,1)} %get-tuple-element.8.anc_ref.prev_ref.own_ref, bf16[4,1024,1152]{2,1,0:T(8,128)(2,1)} %get-tuple-element.8.anc_ref.prev_ref.own_ref, ...), custom_call_target="tpu_custom_call" | custom-call | tf_op jit(solution)/shard_map/attend/pallas_call | solution.py:366
  170.5 0.7 constant_dynamic-slice_fusion.gate_ref
  171.1 1.2 dynamic-slice_bitcast_fusion.res_ref
  172.3 16.4 %project_out.1 = bf16[512,576]{1,0:T(8,128)(2,1)} custom-call(bf16[1024,288]{1,0:T(8,128)(2,1)} %attend.1.att_ref, bf16[2,2,2,288,288]{4,3,2,1,0:T(8,128)(2,1)} %get-tuple-element.10.wo_ref, bf16[512,576]{1,0:T(8,128)(2,1)} %dynamic-slice_bitcast_fusion.res_ref, f32[1,576]{1,0:T(1,128)} %constant_dynamic-slice_fusion.gate_ref), custom_call_target="tpu_custom_call" | custom-call | tf_op jit(solution)/shard_map/project_out/pallas_call | solution.py:426
  188.7 2.1 %copy.11 = bf16[1,512,576]{1,2,0:T(8,128)(2,1)} copy(bf16[1,512,576]{2,1,0:T(8,128)(2,1)} %bitcast.32) | data formatting | bytes 1179648 | tf_op jit(solution)/shard_map/broadcast_in_dim | solution.py:471
  (3 shorter events, 0.0 us)
Async XLA Ops:
  0.0 1.5 copy-start
  0.0 7.5 %copy-start.3 = (f32[3,1152]{1,0:T(4,128)S(1)}, f32[3,1152]{1,0:T(4,128)}, u32[]{:S(2)}) copy-start(f32[3,1152]{1,0:T(4,128)} %param.6) | copy-start | bytes 41476
  0.0 7.5 %copy-start.1 = (bf16[1,512,1152]{2,1,0:T(8,128)(2,1)S(1)}, bf16[1,512,1152]{2,1,0:T(8,128)(2,1)}, u32[]{:S(2)}) copy-start(bf16[1,512,1152]{2,1,0:T(8,128)(2,1)} %param.5) | copy-start | bytes 3538948
  7.5 2.2 %copy-start.2 = (bf16[576,288]{0,1:T(8,128)(2,1)S(1)}, bf16[576,288]{0,1:T(8,128)(2,1)}, u32[]{:S(2)}) copy-start(bf16[576,288]{0,1:T(8,128)(2,1)} %param.8) | copy-start | bytes 995332

commit v2 on v1

--- a/solution.py
+++ b/solution.py
@@ -149,7 +149,8 @@
 
 def gather_kernel(
     nz, h_ref, w_ref, wo_ref, h_all, w_all, wo_all,
-    local_sem, h_send, h_fwd, h_core, h_recv, w_send, w_fwd, w_recv, o_send, o_fwd, o_recv, o_own,
+    local_sem, h_send, h_line, h_fwd, h_core, h_tok, h_tok_own, h_recv, w_send, w_line, w_fwd, w_recv,
+    o_send, o_fwd, o_recv, o_own,
 ):
     y, z = lax.axis_index("groups"), lax.axis_index("frame")
     x, c = lax.axis_index("tok"), lax.axis_index("head")
@@ -179,16 +180,69 @@
     def piece(frame, tok, core):
         return h_all.at[frame, pl.ds((tok * 2 + core) * quarter, quarter)]
 
+    def each_source(visit):
+        for d in range(1, nz):
+            for side, sign in enumerate((-1, 1)):
+                source = z + sign * d
+
+                @pl.when((source >= 0) & (source < nz))
+                def _():
+                    visit(source, (side, d - 1), z - sign)
+
+    def if_inside(frame, act):
+        @pl.when((frame >= 0) & (frame < nz))
+        def _():
+            act()
+
     mine = h_ref.at[pl.ds(c * quarter, quarter)]
+    out = remote(mine, piece(z, x, c), h_send.at[2], h_recv.at[z, x, c], tok=1 - x)
+
+    def first(side, sign):
+        return (
+            remote(mine, piece(z, x, c), h_send.at[side], h_recv.at[z, x, c], frame=z + sign),
+            remote(w_ref.at[y], w_all.at[z, y], w_send.at[side], w_recv.at[z, y], frame=z + sign),
+        )
+
+    def onward_h(source, at, ahead):
+        got = piece(source, x, c)
+        return remote(got, got, h_line.at[at], h_recv.at[source, x, c], frame=ahead)
+
+    def onward_w(source, at, ahead):
+        got = w_all.at[source, y]
+        return remote(got, got, w_line.at[at], w_recv.at[source, y], frame=ahead)
+
+    def across_h(source, at):
+        got = piece(source, x, c)
+        return (
+            remote(got, got, h_fwd.at[at], h_recv.at[source, x, c], tok=1 - x),
+            remote(got, got, h_core.at[at], h_recv.at[source, x, c], head=1 - c),
+        )
+
+    def across_w(source, at):
+        got = w_all.at[source, y]
+        return remote(got, got, w_fwd.at[at], w_recv.at[source, y], groups=1 - y)
+
+    def from_tok(source, sem):
+        got = piece(source, 1 - x, c)
+        return remote(got, got, sem, h_recv.at[source, 1 - x, c], head=1 - c)
+
+    for side, sign in enumerate((-1, 1)):
+        if_inside(z + sign, lambda: [copy.start() for copy in first(side, sign)])
+    out.start()
+
+    def arrived(ref, sem):
+        remote(ref, ref, h_send.at[0], sem, head=1 - c).wait_recv()
+
+    def pass_on(source, at, ahead):
+        arrived(piece(source, x, c), h_recv.at[source, x, c])
+        if_inside(ahead, lambda: onward_h(source, at, ahead).start())
+        for copy in across_h(source, at):
+            copy.start()
+        arrived(w_all.at[source, y], w_recv.at[source, y])
+        if_inside(ahead, lambda: onward_w(source, at, ahead).start())
+        across_w(source, at).start()
+
     sends = []
-    for k, other in enumerate(others):
-        sends.append(remote(mine, piece(z, x, c), h_send.at[k], h_recv.at[z, x, c], frame=other))
-        sends[-1].start()
-    sends.append(remote(mine, piece(z, x, c), h_send.at[nz - 1], h_recv.at[z, x, c], tok=1 - x))
-    sends[-1].start()
-    for k, other in enumerate(others):
-        sends.append(remote(w_ref.at[y], w_all.at[z, y], w_send.at[k], w_recv.at[z, y], frame=other))
-        sends[-1].start()
     for k, other in enumerate(others):
         sends.append(
             remote(wo_ref.at[y], wo_all.at[slot, c, y], o_send.at[k], o_recv.at[slot, c, y], frame=other, head=home)
@@ -200,20 +254,15 @@
     def _():
         over.start()
 
-    def arrived(ref, sem):
-        remote(ref, ref, h_send.at[0], sem, head=1 - c).wait_recv()
-
-    for k, other in enumerate(others):
-        got = piece(other, x, c)
-        arrived(got, h_recv.at[other, x, c])
-        sends.append(remote(got, got, h_fwd.at[k], h_recv.at[other, x, c], tok=1 - x))
-        sends[-1].start()
-        sends.append(remote(got, got, h_core.at[0, k], h_recv.at[other, x, c], head=1 - c))
-        sends[-1].start()
-        part = w_all.at[other, y]
-        arrived(part, w_recv.at[other, y])
-        sends.append(remote(part, part, w_fwd.at[k], w_recv.at[other, y], groups=1 - y))
-        sends[-1].start()
+    each_source(pass_on)
+    arrived(piece(z, 1 - x, c), h_recv.at[z, 1 - x, c])
+    from_tok(z, h_tok_own).start()
+
+    def pass_tok(source, at, ahead):
+        arrived(piece(source, 1 - x, c), h_recv.at[source, 1 - x, c])
+        from_tok(source, h_tok.at[at]).start()
+
+    each_source(pass_tok)
     for i in range(per_core):
         for core in (0, 1):
             block = wo_all.at[i, core, y]
@@ -224,11 +273,6 @@
                 arrived(block, o_recv.at[i, core, y])
                 onward.start()
 
-    for k, frame in enumerate([z] + others):
-        got = piece(frame, 1 - x, c)
-        arrived(got, h_recv.at[frame, 1 - x, c])
-        sends.append(remote(got, got, h_core.at[1, k], h_recv.at[frame, 1 - x, c], head=1 - c))
-        sends[-1].start()
     for other in others:
         arrived(w_all.at[other, 1 - y], w_recv.at[other, 1 - y])
         arrived(piece(other, x, 1 - c), h_recv.at[other, x, 1 - c])
@@ -253,6 +297,20 @@
     def _():
         over.wait_send()
 
+    for side, sign in enumerate((-1, 1)):
+        if_inside(z + sign, lambda: [copy.wait_send() for copy in first(side, sign)])
+    out.wait_send()
+    from_tok(z, h_tok_own).wait_send()
+
+    def finish(source, at, ahead):
+        if_inside(ahead, lambda: onward_h(source, at, ahead).wait_send())
+        if_inside(ahead, lambda: onward_w(source, at, ahead).wait_send())
+        for copy in across_h(source, at):
+            copy.wait_send()
+        across_w(source, at).wait_send()
+        from_tok(source, h_tok.at[at]).wait_send()
+
+    each_source(finish)
     for copy in locals_:
         copy.wait()
     for copy in sends:
@@ -274,12 +332,16 @@
         out_specs=(anywhere,) * 3,
         scratch_shapes=[
             dma((3,)),
-            dma((nz,)),
-            dma((nz - 1,)),
-            dma((2, nz)),
+            dma((3,)),
+            dma((2, nz - 1)),
+            dma((2, nz - 1)),
+            dma((2, nz - 1)),
+            dma((2, nz - 1)),
+            dma,
             dma((nz, 2, 2)),
-            dma((nz - 1,)),
-            dma((nz - 1,)),
+            dma((2,)),
+            dma((2, nz - 1)),
+            dma((2, nz - 1)),
             dma((nz, 2)),
             dma((nz,)),
             dma((nz // 2, 2)),
@@ -294,7 +356,7 @@
 def attend_kernel(heads, hd, chunk, pick, anc_ref, prev_ref, own_ref, w_ref, o_ref, wide, keys, vals, queries):
     step = pl.program_id(0)
     frame_rows = own_ref.shape[1]
-    lanes = keys.shape[2]
+    lanes, depth = keys.shape[2], w_ref.shape[2]
 
     @pl.when(step == 0)
     def _():
@@ -302,12 +364,17 @@
         for head in range(heads):
             for what in range(3):
                 place = ((what + 2) % 3 * heads + head) * lanes
-                wide[:, place : place + hd] = w_ref[:, (head * 3 + what) * hd : (head * 3 + what + 1) * hd]
+                for part in range(w_ref.shape[0]):
+                    wide[place : place + hd, part * depth : (part + 1) * depth] = w_ref[
+                        part, (head * 3 + what) * hd : (head * 3 + what + 1) * hd, :
+                    ]
 
         def project(ref, at, columns, targets, base):
             here = pl.ds(pl.multiple_of(at * chunk, chunk), chunk)
             there = pl.ds(pl.multiple_of(base + at * chunk, chunk), chunk)
-            mixed = jnp.dot(ref[0, here, :], wide[:, columns], preferred_element_type=jnp.float32)
+            mixed = lax.dot_general(
+                ref[0, here, :], wide[columns, :], (((1,), (1,)), ((), ())), preferred_element_type=jnp.float32
+            )
             mixed = mixed.astype(jnp.bfloat16)
             for t, target in enumerate(targets):
                 for head in range(heads):
@@ -369,10 +436,10 @@
         grid_spec=pltpu.PrefetchScalarGridSpec(
             num_scalar_prefetch=1,
             grid=(frame_rows // block_rows,),
-            in_specs=[frame_block(2), frame_block(1), frame_block(0), pl.BlockSpec(weight.shape, lambda i, pick: (0, 0))],
+            in_specs=[frame_block(2), frame_block(1), frame_block(0), pl.BlockSpec(weight.shape, lambda i, pick: (0, 0, 0))],
             out_specs=pl.BlockSpec((block_rows, heads * hd), lambda i, pick: (i, 0)),
             scratch_shapes=[
-                pltpu.VMEM((width, 3 * heads * lanes), jnp.bfloat16),
+                pltpu.VMEM((3 * heads * lanes, width), jnp.bfloat16),
                 pltpu.VMEM((heads, 3 * frame_rows, lanes), jnp.bfloat16),
                 pltpu.VMEM((heads, 3 * frame_rows, lanes), jnp.bfloat16),
                 pltpu.VMEM((heads, frame_rows, lanes), jnp.bfloat16),
@@ -450,8 +517,8 @@
     normed = centred * lax.rsqrt(row_var + 1e-06)
     hidden = (normed * (1.0 + modulation[1]) + modulation[0]).astype(jnp.bfloat16)
     heads = head_local // 2
-    weight = lax.dynamic_slice_in_dim(w_qkv, x * heads, heads, 1)
-    weight = weight.reshape(2, depth // 2, heads * 3 * head_dim)
+    weight = lax.dynamic_slice_in_dim(jnp.transpose(w_qkv, (1, 2, 3, 0)), x * heads, heads, 0)
+    weight = weight.reshape(2, heads * 3 * head_dim // 2, depth)
     out_weight = w_out.reshape(2, w_out.shape[0] // 2, w_out.shape[1])
     h_all, w_all, wo_all = gather(hidden, weight, out_weight, nz)
     anchor = anchor_offsets[0]
@@ -464,7 +531,7 @@
             (z > 0).astype(jnp.int32),
         ]
     ).astype(jnp.int32)
-    attended = attend_heads(pick, h_all, w_all.reshape(model_width, heads * 3 * head_dim), heads, head_dim)
+    attended = attend_heads(pick, h_all, w_all.reshape(nz, heads * 3 * head_dim, depth), heads, head_dim)
     half_width = model_width // 2
     residual = lax.dynamic_slice_in_dim(rows, c * half_width, half_width, 1)
     gate = lax.dynamic_slice_in_dim(modulation[2:3], c * half_width, half_width, 1)

time: 191 us -> 172 us (0.901)
  the two profiles are of different devices: /device:TPU:9 before, /device:TPU:0 now
where the time goes in v2:
time: 172 us; the launch traced here: 171 us
  Pallas kernels  159 us (92%)
  local copies, waits for them, and re-layouts  6.51 us (4%)
  other arithmetic  4.41 us (3%)
    pallas_call x1, Pallas kernels, gather(): pl.pallas_call(functools.partial(gather_kernel, nz), out_shape=(jax.Shape...  103 us
    pallas_call x1, Pallas kernels, attend_heads(): pl.pallas_call(functools.partial(attend_kernel, heads, hd, block_rows), o...  38 us
    pallas_call x1, Pallas kernels, project_out(): pl.pallas_call(functools.partial(output_kernel, out_weight.shape[0]), out...  18.3 us

profile of v2, /device:TPU:0, one launch (start us, length us, event | category | flops | bytes accessed | tf_op | source)
XLA Modules:
  0.0 171.1 jit_solution(16403713702673553767)
XLA Ops:
  0.0 0.0 copy-start
  0.0 0.0 copy-start.1
  0.8 0.6 stack.27.pick
  1.4 0.0 copy-done
  1.5 0.9 constant_dynamic-slice_fusion.1
  2.4 0.9 add_reduce_fusion
  3.2 0.0 copy-start.2
  3.2 1.5 convert_reduce_fusion
  4.8 0.0 copy-done.1
  4.8 0.4 fusion.3
  5.3 1.5 fusion.6.h_ref
  6.8 0.0 copy-done.2
  6.8 1.0 copy.6
  7.8 103.0 %gather.1 = (bf16[4,1024,1152]{2,1,0:T(8,128)(2,1)}, bf16[4,2,432,288]{3,2,1,0:T(8,128)(2,1)}, bf16[2,2,2,288,288]{4,3,2,1,0:T(8,128)(2,1)}) custom-call(bf16[512,1152]{1,0:T(8,128)(2,1)} %fusion.6.h_ref, bf16[2,432,288]{2,1,0:T(8,128)(2,1)} %bitcast.32, bf16[2,288,288]{2,1,0:T(8,128)(2,1)} %bitcast.34), custom_call_target="tpu_custom_call" | custom-call | tf_op jit(solution)/shard_map/gather/pallas_call | solution.py:324
  110.8 38.0 %attend.1.att_ref = bf16[1024,288]{1,0:T(8,128)(2,1)} custom-call(s32[5]{0:T(128)} %stack.27.pick, bf16[4,1024,1152]{2,1,0:T(8,128)(2,1)} %get-tuple-element.8.anc_ref.prev_ref.own_ref, bf16[4,1024,1152]{2,1,0:T(8,128)(2,1)} %get-tuple-element.8.anc_ref.prev_ref.own_ref, bf16[4,1024,1152]{2,1,0:T(8,128)(2,1)} %get-tuple-element.8.anc_ref.prev_ref.own_ref, ...), custom_call_target="tpu_custom_call" | custom-call | tf_op jit(solution)/shard_map/attend/pallas_call | solution.py:433
  148.8 0.7 constant_dynamic-slice_fusion.gate_ref
  149.5 1.2 dynamic-slice_bitcast_fusion.res_ref
  150.7 18.3 %project_out.1 = bf16[512,576]{1,0:T(8,128)(2,1)} custom-call(bf16[1024,288]{1,0:T(8,128)(2,1)} %attend.1.att_ref, bf16[2,2,2,288,288]{4,3,2,1,0:T(8,128)(2,1)} %get-tuple-element.10.wo_ref, bf16[512,576]{1,0:T(8,128)(2,1)} %dynamic-slice_bitcast_fusion.res_ref, f32[1,576]{1,0:T(1,128)} %constant_dynamic-slice_fusion.gate_ref), custom_call_target="tpu_custom_call" | custom-call | tf_op jit(solution)/shard_map/project_out/pallas_call | solution.py:493
  169.0 2.1 %copy.7 = bf16[1,512,576]{1,2,0:T(8,128)(2,1)} copy(bf16[1,512,576]{2,1,0:T(8,128)(2,1)} %bitcast.33) | data formatting | bytes 1179648 | tf_op jit(solution)/shard_map/broadcast_in_dim | solution.py:538
  (2 shorter events, 0.0 us)
Async XLA Ops:
  0.0 1.5 copy-start
  0.0 4.8 %copy-start.1 = (bf16[1,512,1152]{2,1,0:T(8,128)(2,1)S(1)}, bf16[1,512,1152]{2,1,0:T(8,128)(2,1)}, u32[]{:S(2)}) copy-start(bf16[1,512,1152]{2,1,0:T(8,128)(2,1)} %param.5) | copy-start | bytes 3538948
  3.2 3.6 %copy-start.2 = (bf16[576,288]{0,1:T(8,128)(2,1)S(1)}, bf16[576,288]{0,1:T(8,128)(2,1)}, u32[]{:S(2)}) copy-start(bf16[576,288]{0,1:T(8,128)(2,1)} %param.8) | copy-start | bytes 995332

commit v3 on v2

--- a/solution.py
+++ b/solution.py
@@ -148,7 +148,7 @@
 
 
 def gather_kernel(
-    nz, h_ref, w_ref, wo_ref, h_all, w_all, wo_all,
+    nz, heads, hd, h_ref, w_ref, wo_ref, queries, keys, vals, wo_all, h_all, w_all, wide,
     local_sem, h_send, h_line, h_fwd, h_core, h_tok, h_tok_own, h_recv, w_send, w_line, w_fwd, w_recv,
     o_send, o_fwd, o_recv, o_own,
 ):
@@ -180,8 +180,8 @@
     def piece(frame, tok, core):
         return h_all.at[frame, pl.ds((tok * 2 + core) * quarter, quarter)]
 
-    def each_source(visit):
-        for d in range(1, nz):
+    def each_source(visit, steps=range(1, nz)):
+        for d in steps:
             for side, sign in enumerate((-1, 1)):
                 source = z + sign * d
 
@@ -197,11 +197,11 @@
     mine = h_ref.at[pl.ds(c * quarter, quarter)]
     out = remote(mine, piece(z, x, c), h_send.at[2], h_recv.at[z, x, c], tok=1 - x)
 
-    def first(side, sign):
-        return (
-            remote(mine, piece(z, x, c), h_send.at[side], h_recv.at[z, x, c], frame=z + sign),
-            remote(w_ref.at[y], w_all.at[z, y], w_send.at[side], w_recv.at[z, y], frame=z + sign),
-        )
+    def first_h(side, sign):
+        return remote(mine, piece(z, x, c), h_send.at[side], h_recv.at[z, x, c], frame=z + sign)
+
+    def first_w(side, sign):
+        return remote(w_ref.at[y], w_all.at[z, y], w_send.at[side], w_recv.at[z, y], frame=z + sign)
 
     def onward_h(source, at, ahead):
         got = piece(source, x, c)
@@ -226,43 +226,95 @@
         got = piece(source, 1 - x, c)
         return remote(got, got, sem, h_recv.at[source, 1 - x, c], head=1 - c)
 
-    for side, sign in enumerate((-1, 1)):
-        if_inside(z + sign, lambda: [copy.start() for copy in first(side, sign)])
-    out.start()
-
     def arrived(ref, sem):
         remote(ref, ref, h_send.at[0], sem, head=1 - c).wait_recv()
 
-    def pass_on(source, at, ahead):
+    def pass_h(source, at, ahead):
         arrived(piece(source, x, c), h_recv.at[source, x, c])
         if_inside(ahead, lambda: onward_h(source, at, ahead).start())
         for copy in across_h(source, at):
             copy.start()
+
+    def pass_w(source, at, ahead):
         arrived(w_all.at[source, y], w_recv.at[source, y])
         if_inside(ahead, lambda: onward_w(source, at, ahead).start())
         across_w(source, at).start()
 
-    sends = []
-    for k, other in enumerate(others):
-        sends.append(
-            remote(wo_ref.at[y], wo_all.at[slot, c, y], o_send.at[k], o_recv.at[slot, c, y], frame=other, head=home)
-        )
-        sends[-1].start()
+    def pass_tok(source, at, ahead):
+        arrived(piece(source, 1 - x, c), h_recv.at[source, 1 - x, c])
+        from_tok(source, h_tok.at[at]).start()
+
+    sends = [
+        remote(wo_ref.at[y], wo_all.at[slot, c, y], o_send.at[k], o_recv.at[slot, c, y], frame=other, head=home)
+        for k, other in enumerate(others)
+    ]
     over = remote(wo_ref, wo_all.at[slot, c], o_send.at[nz - 1], o_own, head=1 - c)
+
+    lanes, depth, chunk = keys.shape[3], w_ref.shape[2], math.gcd(256, keys.shape[2])
+
+    def project(frame, columns, targets):
+        @pl.loop(0, h_all.shape[1] // chunk)
+        def _(at):
+            here = pl.ds(pl.multiple_of(at * chunk, chunk), chunk)
+            mixed = lax.dot_general(
+                h_all[frame, here, :], wide[columns, :], (((1,), (1,)), ((), ())), preferred_element_type=jnp.float32
+            ).astype(jnp.bfloat16)
+            for t, target in enumerate(targets):
+                for head in range(heads):
+                    place = (t * heads + head) * lanes
+                    target[head, here, :] = mixed[:, place : place + lanes]
+
+    both = slice(0, 2 * heads * lanes)
+
+    def project_source(source, at, ahead):
+        arrived(piece(source, x, 1 - c), h_recv.at[source, x, 1 - c])
+        arrived(piece(source, 1 - x, 1 - c), h_recv.at[source, 1 - x, 1 - c])
+        project(source, both, (keys.at[source], vals.at[source]))
+
+    for side, sign in enumerate((-1, 1)):
+        if_inside(z + sign, lambda: first_w(side, sign).start())
+        if_inside(z + sign, lambda: first_h(side, sign).start())
+    out.start()
+    wide[...] = jnp.zeros_like(wide)
+    for d in range(1, nz):
+        each_source(pass_w, [d])
+        if d < nz - 1 or d == 1:
+            each_source(pass_h, [d])
+        if d == 1:
+            arrived(piece(z, 1 - x, c), h_recv.at[z, 1 - x, c])
+            from_tok(z, h_tok_own).start()
+        else:
+            each_source(pass_tok, [d - 1])
+    for other in others:
+        arrived(w_all.at[other, 1 - y], w_recv.at[other, 1 - y])
+    for copy in locals_:
+        copy.wait()
+    half = w_ref.shape[1]
+    for head in range(heads):
+        for what in range(3):
+            place = ((what + 2) % 3 * heads + head) * lanes
+            low = (head * 3 + what) * hd
+            at, low = low // half, low % half
+            for part in range(nz):
+                wide[place : place + hd, part * depth : (part + 1) * depth] = w_all[part, at, low : low + hd, :]
+    arrived(piece(z, 1 - x, 1 - c), h_recv.at[z, 1 - x, 1 - c])
+    project(z, slice(2 * heads * lanes, 3 * heads * lanes), (queries,))
+    for copy in sends:
+        copy.start()
 
     @pl.when(home != c)
     def _():
         over.start()
 
-    each_source(pass_on)
-    arrived(piece(z, 1 - x, c), h_recv.at[z, 1 - x, c])
-    from_tok(z, h_tok_own).start()
-
-    def pass_tok(source, at, ahead):
-        arrived(piece(source, 1 - x, c), h_recv.at[source, 1 - x, c])
-        from_tok(source, h_tok.at[at]).start()
-
-    each_source(pass_tok)
+    project(z, both, (keys.at[z], vals.at[z]))
+    for d in range(1, nz - 2):
+        each_source(project_source, [d])
+    if nz > 2:
+        each_source(pass_h, [nz - 1])
+    for d in range(max(1, nz - 2), nz - 1):
+        each_source(project_source, [d])
+    each_source(pass_tok, [nz - 1])
+    each_source(project_source, [nz - 1])
     for i in range(per_core):
         for core in (0, 1):
             block = wo_all.at[i, core, y]
@@ -273,11 +325,6 @@
                 arrived(block, o_recv.at[i, core, y])
                 onward.start()
 
-    for other in others:
-        arrived(w_all.at[other, 1 - y], w_recv.at[other, 1 - y])
-        arrived(piece(other, x, 1 - c), h_recv.at[other, x, 1 - c])
-    for frame in [z] + others:
-        arrived(piece(frame, 1 - x, 1 - c), h_recv.at[frame, 1 - x, 1 - c])
     for i in range(per_core):
         for core in (0, 1):
             block = wo_all.at[i, core, y]
@@ -298,7 +345,8 @@
         over.wait_send()
 
     for side, sign in enumerate((-1, 1)):
-        if_inside(z + sign, lambda: [copy.wait_send() for copy in first(side, sign)])
+        if_inside(z + sign, lambda: first_h(side, sign).wait_send())
+        if_inside(z + sign, lambda: first_w(side, sign).wait_send())
     out.wait_send()
     from_tok(z, h_tok_own).wait_send()
 
@@ -311,26 +359,30 @@
         from_tok(source, h_tok.at[at]).wait_send()
 
     each_source(finish)
-    for copy in locals_:
-        copy.wait()
     for copy in sends:
         copy.wait_send()
 
 
-def gather(hidden, weight, out_weight, nz):
+def gather(hidden, weight, out_weight, nz, heads, hd):
     rows, width = hidden.shape
+    lanes = -(-hd // 128) * 128
     dma = pltpu.SemaphoreType.DMA
     vmem, anywhere = pl.BlockSpec(memory_space=pltpu.VMEM), pl.BlockSpec(memory_space=pl.ANY)
+    per_frame = jax.ShapeDtypeStruct((nz, heads, 2 * rows, lanes), hidden.dtype)
     return pl.pallas_call(
-        functools.partial(gather_kernel, nz),
+        functools.partial(gather_kernel, nz, heads, hd),
         out_shape=(
-            jax.ShapeDtypeStruct((nz, 2 * rows, width), hidden.dtype),
-            jax.ShapeDtypeStruct((nz,) + weight.shape, weight.dtype),
+            jax.ShapeDtypeStruct((heads, 2 * rows, lanes), hidden.dtype),
+            per_frame,
+            per_frame,
             jax.ShapeDtypeStruct((nz // 2, 2) + out_weight.shape, out_weight.dtype),
         ),
         in_specs=[vmem] * 3,
-        out_specs=(anywhere,) * 3,
+        out_specs=(vmem, vmem, vmem, anywhere),
         scratch_shapes=[
+            pltpu.VMEM((nz, 2 * rows, width), hidden.dtype),
+            pltpu.VMEM((nz,) + weight.shape, weight.dtype),
+            pltpu.VMEM((3 * heads * lanes, width), weight.dtype),
             dma((3,)),
             dma((3,)),
             dma((2, nz - 1)),
@@ -348,60 +400,23 @@
             dma((nz // 2, 2, 2)),
             dma,
         ],
-        compiler_params=pltpu.CompilerParams(collective_id=0, has_side_effects=True),
+        compiler_params=pltpu.CompilerParams(
+            collective_id=0, has_side_effects=True, vmem_limit_bytes=56 * 1024 * 1024
+        ),
         name="gather",
     )(hidden, weight, out_weight)
 
 
-def attend_kernel(heads, hd, chunk, pick, anc_ref, prev_ref, own_ref, w_ref, o_ref, wide, keys, vals, queries):
-    step = pl.program_id(0)
-    frame_rows = own_ref.shape[1]
-    lanes, depth = keys.shape[2], w_ref.shape[2]
-
-    @pl.when(step == 0)
-    def _():
-        wide[...] = jnp.zeros_like(wide)
-        for head in range(heads):
-            for what in range(3):
-                place = ((what + 2) % 3 * heads + head) * lanes
-                for part in range(w_ref.shape[0]):
-                    wide[place : place + hd, part * depth : (part + 1) * depth] = w_ref[
-                        part, (head * 3 + what) * hd : (head * 3 + what + 1) * hd, :
-                    ]
-
-        def project(ref, at, columns, targets, base):
-            here = pl.ds(pl.multiple_of(at * chunk, chunk), chunk)
-            there = pl.ds(pl.multiple_of(base + at * chunk, chunk), chunk)
-            mixed = lax.dot_general(
-                ref[0, here, :], wide[columns, :], (((1,), (1,)), ((), ())), preferred_element_type=jnp.float32
-            )
-            mixed = mixed.astype(jnp.bfloat16)
-            for t, target in enumerate(targets):
-                for head in range(heads):
-                    place = (t * heads + head) * lanes
-                    target[head, there, :] = mixed[:, place : place + lanes]
-
-        both = slice(0, 2 * heads * lanes)
-        for block, ref in enumerate((anc_ref, prev_ref, own_ref)):
-
-            @pl.loop(0, frame_rows // chunk)
-            def _(at):
-                project(ref, at, both, (keys, vals), block * frame_rows)
-
-        @pl.loop(0, frame_rows // chunk)
-        def _(at):
-            project(own_ref, at, slice(2 * heads * lanes, 3 * heads * lanes), (queries,), 0)
-
+def attend_kernel(hd, pick, q_ref, ka_ref, kp_ref, ko_ref, va_ref, vp_ref, vo_ref, o_ref):
+    keys, vals = (ka_ref, kp_ref, ko_ref), (va_ref, vp_ref, vo_ref)
     rate = hd ** (-0.5) * math.log2(math.e)
     offsets = [jnp.where(pick[3 + k] == 1, 0.0, -1e30).astype(jnp.float32) for k in range(2)] + [0.0]
-    rows = o_ref.shape[0]
-    here = pl.ds(pl.multiple_of(step * rows, rows), rows)
-    for head in range(heads):
-        query = queries[head, here, :]
+    for head in range(q_ref.shape[0]):
+        query = q_ref[head]
         scores = [
             lax.dot_general(
                 query,
-                keys[head, k * frame_rows : (k + 1) * frame_rows, :],
+                keys[k][0, head],
                 (((1,), (1,)), ((), ())),
                 preferred_element_type=jnp.float32,
             )
@@ -415,39 +430,33 @@
             denominator += jnp.sum(probs, axis=-1, keepdims=True)
             numerator += jnp.dot(
                 probs.astype(jnp.bfloat16),
-                vals[head, k * frame_rows : (k + 1) * frame_rows, :],
+                vals[k][0, head],
                 preferred_element_type=jnp.float32,
             )
         result = (numerator / denominator).astype(jnp.bfloat16)
         o_ref[:, head * hd : (head + 1) * hd] = result[:, :hd]
 
 
-def attend_heads(pick, h_all, weight, heads, hd):
-    _, frame_rows, width = h_all.shape
-    lanes = -(-hd // 128) * 128
+def attend_heads(pick, queries, keys, vals, hd):
+    _, heads, frame_rows, lanes = keys.shape
     block_rows = math.gcd(256, frame_rows)
 
     def frame_block(which):
-        return pl.BlockSpec((1, frame_rows, width), lambda i, pick: (pick[which], 0, 0))
-
+        return pl.BlockSpec((1, heads, frame_rows, lanes), lambda i, pick: (pick[which], 0, 0, 0))
+
+    blocks = [frame_block(which) for which in (2, 1, 0)]
     return pl.pallas_call(
-        functools.partial(attend_kernel, heads, hd, block_rows),
+        functools.partial(attend_kernel, hd),
         out_shape=jax.ShapeDtypeStruct((frame_rows, heads * hd), jnp.bfloat16),
         grid_spec=pltpu.PrefetchScalarGridSpec(
             num_scalar_prefetch=1,
             grid=(frame_rows // block_rows,),
-            in_specs=[frame_block(2), frame_block(1), frame_block(0), pl.BlockSpec(weight.shape, lambda i, pick: (0, 0, 0))],
+            in_specs=[pl.BlockSpec((heads, block_rows, lanes), lambda i, pick: (0, i, 0))] + blocks * 2,
             out_specs=pl.BlockSpec((block_rows, heads * hd), lambda i, pick: (i, 0)),
-            scratch_shapes=[
-                pltpu.VMEM((3 * heads * lanes, width), jnp.bfloat16),
-                pltpu.VMEM((heads, 3 * frame_rows, lanes), jnp.bfloat16),
-                pltpu.VMEM((heads, 3 * frame_rows, lanes), jnp.bfloat16),
-                pltpu.VMEM((heads, frame_rows, lanes), jnp.bfloat16),
-            ],
         ),
-        compiler_params=pltpu.CompilerParams(vmem_limit_bytes=56 * 1024 * 1024),
+        compiler_params=pltpu.CompilerParams(vmem_limit_bytes=48 * 1024 * 1024),
         name="attend",
-    )(pick, h_all, h_all, h_all, weight)
+    )(pick, queries, keys, keys, keys, vals, vals, vals)
 
 
 def output_kernel(per_core, att_ref, wo_ref, res_ref, gate_ref, o_ref, held, send, recv):
@@ -520,7 +529,7 @@
     weight = lax.dynamic_slice_in_dim(jnp.transpose(w_qkv, (1, 2, 3, 0)), x * heads, heads, 0)
     weight = weight.reshape(2, heads * 3 * head_dim // 2, depth)
     out_weight = w_out.reshape(2, w_out.shape[0] // 2, w_out.shape[1])
-    h_all, w_all, wo_all = gather(hidden, weight, out_weight, nz)
+    queries, keys, vals, wo_all = gather(hidden, weight, out_weight, nz, heads, head_dim)
     anchor = anchor_offsets[0]
     pick = jnp.stack(
         [
@@ -531,7 +540,7 @@
             (z > 0).astype(jnp.int32),
         ]
     ).astype(jnp.int32)
-    attended = attend_heads(pick, h_all, w_all.reshape(nz, heads * 3 * head_dim, depth), heads, head_dim)
+    attended = attend_heads(pick, queries, keys, vals, head_dim)
     half_width = model_width // 2
     residual = lax.dynamic_slice_in_dim(rows, c * half_width, half_width, 1)
     gate = lax.dynamic_slice_in_dim(modulation[2:3], c * half_width, half_width, 1)

time: 172 us -> 165 us (0.959)
  Pallas kernels: 159 us -> 149 us
  local copies, waits for them, and re-layouts: 6.51 us -> 10.7 us
    pallas_call x2, Pallas kernels: 141 us -> 128 us  [the longest x1 106 us: gather(): pl.pallas_call(functools.partial(gather_kernel, nz, heads, hd), out_shape...]
    unnamed x7 -> x13, local copies, waits for them, and re-layouts: 0.97 us -> 5.69 us
    pallas_call x1, Pallas kernels: 18.3 us -> 21 us  [project_out(): pl.pallas_call(functools.partial(output_kernel, out_weight.shape[0]), out...]
where the time goes in v3:
time: 165 us
  Pallas kernels  149 us (90%)
  local copies, waits for them, and re-layouts  10.7 us (6%)
  other arithmetic  4.4 us (3%)
    pallas_call x1, Pallas kernels, gather(): pl.pallas_call(functools.partial(gather_kernel, nz, heads, hd), out_shape...  106 us
    pallas_call x1, Pallas kernels, attend_heads(): pl.pallas_call(functools.partial(attend_kernel, hd), out_shape=jax.ShapeD...  21.4 us
    pallas_call x1, Pallas kernels, project_out(): pl.pallas_call(functools.partial(output_kernel, out_weight.shape[0]), out...  21 us
    unnamed x13, local copies, waits for them, and re-layouts  5.69 us

profile of v3, /device:TPU:0, one launch (start us, length us, event | category | flops | bytes accessed | tf_op | source)
XLA Modules:
  0.0 164.7 jit_solution(14191372560019306398)
XLA Ops:
  0.0 0.0 copy-start
  0.0 0.0 copy-start.4
  0.8 0.1 stack.27.pick
  0.9 0.4 copy-done
  1.3 0.9 constant_dynamic-slice_fusion.1
  2.3 0.9 add_reduce_fusion
  3.1 0.0 copy-start.5
  3.1 1.5 convert_reduce_fusion
  4.7 0.0 copy-done.4
  4.7 0.4 fusion.3
  5.2 1.5 fusion.6.h_ref
  6.7 0.0 copy-done.5
  6.7 1.0 copy.6
  7.7 106.3 %gather.1 = (bf16[4,1024,128]{2,1,0:T(8,128)(2,1)}, bf16[4,4,1024,128]{3,2,1,0:T(8,128)(2,1)}, bf16[4,4,1024,128]{3,2,1,0:T(8,128)(2,1)}, bf16[2,2,2,288,288]{4,3,2,1,0:T(8,128)(2,1)}) custom-call(bf16[512,1152]{1,0:T(8,128)(2,1)} %fusion.6.h_ref, bf16[2,432,288]{2,1,0:T(8,128)(2,1)} %bitcast.30, bf16[2,288,288]{2,1,0:T(8,128)(2,1)} %bitcast.32), custom_call_target="tpu_custom_call" | custom-call | tf_op jit(solution)/shard_map/gather/pallas_call | solution.py:372
  114.0 0.0 copy-start.1
  114.0 2.2 %copy-done.1 = bf16[4,4,1024,128]{3,2,1,0:T(8,128)(2,1)S(1)} copy-done((bf16[4,4,1024,128]{3,2,1,0:T(8,128)(2,1)S(1)}, bf16[4,4,1024,128]{3,2,1,0:T(8,128)(2,1)}, u32[]{:S(2)}) %copy-start.1) | copy-done | bytes 4194328
  116.2 0.0 copy-start.3
  116.2 1.2 copy-done.3
  117.4 21.4 %attend.1.att_ref = bf16[1024,288]{1,0:T(8,128)(2,1)S(1)} custom-call(s32[5]{0:T(128)S(1)} %stack.27.pick, bf16[4,1024,128]{2,1,0:T(8,128)(2,1)S(1)} %copy-done.3, bf16[4,4,1024,128]{3,2,1,0:T(8,128)(2,1)S(1)} %copy-done.1, bf16[4,4,1024,128]{3,2,1,0:T(8,128)(2,1)S(1)} %copy-done.1, bf16[4,4,1024,128]{3,2,1,0:T(8,128)(2,1)S(1)} %copy-done.1, ...), custom_call_target="tpu_custom_call" | custom-call | tf_op jit(solution)/shard_map/attend/pallas_call | solution.py:448
  138.8 0.0 copy-start.2
  138.8 0.9 copy-done.2
  139.7 0.7 constant_dynamic-slice_fusion.gate_ref
  140.3 1.2 dynamic-slice_bitcast_fusion.res_ref
  141.6 21.0 %project_out.1 = bf16[512,576]{1,0:T(8,128)(2,1)} custom-call(bf16[1024,288]{1,0:T(8,128)(2,1)} %copy-done.2, bf16[2,2,2,288,288]{4,3,2,1,0:T(8,128)(2,1)} %get-tuple-element.12.wo_ref, bf16[512,576]{1,0:T(8,128)(2,1)} %dynamic-slice_bitcast_fusion.res_ref, f32[1,576]{1,0:T(1,128)} %constant_dynamic-slice_fusion.gate_ref), custom_call_target="tpu_custom_call" | custom-call | tf_op jit(solution)/shard_map/project_out/pallas_call | solution.py:502
  162.5 2.1 %copy.7 = bf16[1,512,576]{1,2,0:T(8,128)(2,1)} copy(bf16[1,512,576]{2,1,0:T(8,128)(2,1)} %bitcast.31) | data formatting | bytes 1179648 | tf_op jit(solution)/shard_map/broadcast_in_dim | solution.py:547
  (2 shorter events, 0.0 us)
Async XLA Ops:
  0.0 1.3 copy-start
  0.0 4.7 %copy-start.4 = (bf16[1,512,1152]{2,1,0:T(8,128)(2,1)S(1)}, bf16[1,512,1152]{2,1,0:T(8,128)(2,1)}, u32[]{:S(2)}) copy-start(bf16[1,512,1152]{2,1,0:T(8,128)(2,1)} %param.5) | copy-start | bytes 3538948
  3.1 3.6 %copy-start.5 = (bf16[576,288]{0,1:T(8,128)(2,1)S(1)}, bf16[576,288]{0,1:T(8,128)(2,1)}, u32[]{:S(2)}) copy-start(bf16[576,288]{0,1:T(8,128)(2,1)} %param.8) | copy-start | bytes 995332
  114.0 2.2 %copy-start.1 = (bf16[4,4,1024,128]{3,2,1,0:T(8,128)(2,1)S(1)}, bf16[4,4,1024,128]{3,2,1,0:T(8,128)(2,1)}, u32[]{:S(2)}) copy-start(bf16[4,4,1024,128]{3,2,1,0:T(8,128)(2,1)} %get-tuple-element.10.ka_ref.kp_ref.ko_ref) | copy-start | bytes 12582916
  116.2 1.2 copy-start.3
  138.8 0.9 copy-start.2
